TPU v7x, 32 devices: a whole 2x2x4 slice. The times are simulated.
32 devices in a mesh: rows: 8 (over z, y), vocab: 4 (over x, core).
Axes of the slice: x: 2, y: 2, z: 4, core: 2. Of those that a mesh axis runs over, the one named last changes fastest.
Arguments:
- hidden_policy: bfloat16 [512, 1536], P('rows', 'vocab'), may hold values from -45 to 45
- hidden_reference: bfloat16 [512, 1536], P('rows', 'vocab'), may hold values from -45 to 45
- gain_policy: bfloat16 [1536], replicated, may hold values from 0.5 to 1.5
- gain_reference: bfloat16 [1536], replicated, may hold values from 0.5 to 1.5
- head_policy: bfloat16 [1536, 16384], P(None, ('rows', 'vocab')), may hold values from -20 to 20
- head_reference: bfloat16 [1536, 16384], P(None, ('rows', 'vocab')), may hold values from -20 to 20
- targets: int32 [512], P('rows'), may hold values from 0 to 16383
- loss_mask: int32 [512], P('rows'), may hold values from 0 to 1, as said below
- doc_lengths: int32 [16], replicated, may hold values from 1 to 127, as said below
- doc_owner: int32 [16], replicated, may hold values from 0 to 7, as said below
- doc_score: float32 [16], replicated, may hold values from -3 to 6
Outputs:
- token_logprob: float32 [1024], P('rows')
- doc_advantage: float32 [16], P('rows')
Inputs may be any that keep to these rules, and one draw needn't show every extreme that they name: `loss_mask`: each index of rows holds at most 32 ones among its 64 tokens, and some index holds exactly 32. `doc_lengths`: documents lie end to end in the pack in this order; their lengths add up to 512. `doc_owner`: every index of rows owns exactly 2 documents, whose lengths add up to at most 128; for some index they add up to exactly 128.
All inputs are finite; a program needn't handle non-finite values.
Results may differ from a plain program's by a relative error of at most 0.0025.
Values may be sent and summed in bfloat16 or wider, within the bound.
A program may use at most 128 MiB of HBM per device.

v0:
```python
import jax
import jax.numpy as jnp
from jax import lax
from jax.sharding import PartitionSpec as P

DOC_DEV = 2
CAP = 128
epsilon = 1e-06
kl_weight = 0.1


def merged_2(part, axis, combine):
    gathered = jax.tree.map(lambda a: lax.all_gather(a, axis), part)

    def take(source):
        return jax.tree.map(lambda a: lax.dynamic_index_in_dim(a, source, 0, False), gathered)

    return lax.fori_loop(
        1, lax.axis_size(axis), lambda source, state: combine(state, take(source)), take(0)
    )


def final_norm(hidden, gain_vector):
    values = hidden.astype(jnp.float32)
    inverse_rms = lax.rsqrt(jnp.mean(values * values, axis=1, keepdims=True) + epsilon)
    return (values * inverse_rms * gain_vector.astype(jnp.float32)[None, :]).astype(jnp.bfloat16)


def column_stats(normed, head_shard, target_ids, column_base):
    logits = jnp.dot(normed, head_shard, preferred_element_type=jnp.float32)
    highest = jnp.max(logits, axis=1)
    exp_total = jnp.sum(jnp.exp(logits - highest[:, None]), axis=1)
    columns = jnp.arange(head_shard.shape[1], dtype=jnp.int32)[None, :] + column_base
    target_logit = jnp.sum(jnp.where(columns == target_ids[:, None], logits, 0.0), axis=1)
    return (highest, exp_total, target_logit)


def combine_stats(earlier, latter):
    merged = []
    for member in (0, 3):
        highest = jnp.maximum(earlier[member], latter[member])
        exp_total = earlier[member + 1] * jnp.exp(earlier[member] - highest) + latter[
            member + 1
        ] * jnp.exp(latter[member] - highest)
        merged.extend([highest, exp_total, earlier[member + 2] + latter[member + 2]])
    return tuple(merged)


def fold_sources(arrived):
    reduced = []
    for member in (0, 3):
        highest = jnp.max(arrived[member], axis=0)
        exp_total = jnp.sum(
            arrived[member + 1] * jnp.exp(arrived[member] - highest[None, :]), axis=0
        )
        reduced.extend([highest, exp_total, jnp.sum(arrived[member + 2], axis=0)])
    return tuple(reduced)


def doc_tables(doc_lengths, doc_owner):
    starts = jnp.cumsum(doc_lengths) - doc_lengths
    doc_order = jnp.arange(doc_lengths.shape[0], dtype=jnp.int32)
    before = (
        (doc_owner[None, :] == doc_owner[:, None]) & (doc_order[None, :] < doc_order[:, None])
    ).astype(jnp.int32)
    offset = jnp.sum(before * doc_lengths[None, :], axis=1)
    doc_rank = jnp.sum(before, axis=1)
    return (starts, offset, doc_rank)


def slot_table(owner_index, starts, offset, doc_rank, doc_lengths, doc_owner, slot_count):
    slot_index = jnp.arange(slot_count, dtype=jnp.int32)[:, None]
    inside = (
        (doc_owner[None, :] == owner_index)
        & (slot_index >= offset[None, :])
        & (slot_index < offset[None, :] + doc_lengths[None, :])
    ).astype(jnp.int32)
    slot_token = jnp.sum(inside * (starts[None, :] + slot_index - offset[None, :]), axis=1)
    slot_filled = jnp.sum(inside, axis=1)
    slot_doc = jnp.sum(inside * doc_rank[None, :], axis=1)
    return (slot_token, slot_filled, slot_doc)


def document_rewards(
    policy_lp,
    reference_lp,
    slot_mask,
    slot_doc,
    owner_index,
    doc_owner,
    doc_rank,
    doc_score,
    doc_slots,
):
    weights_mask = slot_mask.astype(jnp.float32)
    log_ratio = policy_lp - reference_lp
    kl_term = 0.5 * log_ratio * log_ratio
    doc_number = jnp.arange(doc_slots, dtype=jnp.int32)[:, None]
    doc_pick = (slot_doc[None, :] == doc_number).astype(jnp.float32)
    counts = jnp.sum(doc_pick * weights_mask[None, :], axis=1)
    kl_sum = jnp.sum(doc_pick * (weights_mask * kl_term)[None, :], axis=1)
    chosen = ((doc_owner[None, :] == owner_index) & (doc_rank[None, :] == doc_number)).astype(
        jnp.float32
    )
    doc_value = jnp.sum(chosen * doc_score[None, :], axis=1)
    reward = doc_value - kl_weight * kl_sum / jnp.maximum(counts, 1.0)
    return (reward, counts)


def per_device(
    hidden_policy,
    hidden_reference,
    gain_policy,
    gain_reference,
    head_policy,
    head_reference,
    targets,
    loss_mask,
    doc_lengths,
    doc_owner,
    doc_score,
):
    row_devices = lax.axis_size("rows")
    tok_dev = targets.shape[0]
    features = (
        lax.all_gather(hidden_policy, "vocab", axis=1, tiled=True),
        lax.all_gather(hidden_reference, "vocab", axis=1, tiled=True),
    )
    normed_policy = final_norm(features[0], gain_policy)
    normed_reference = final_norm(features[1], gain_reference)
    all_targets, all_mask = (
        lax.all_gather(targets, "rows", axis=0, tiled=True),
        lax.all_gather(loss_mask, "rows", axis=0, tiled=True),
    )
    column_base = lax.axis_index(("rows", "vocab")) * head_policy.shape[1]
    piece_stats = column_stats(
        lax.all_gather(normed_policy, "rows", axis=0, tiled=True),
        head_policy,
        all_targets,
        column_base,
    ) + column_stats(
        lax.all_gather(normed_reference, "rows", axis=0, tiled=True),
        head_reference,
        all_targets,
        column_base,
    )
    statistics = tuple((update for update in piece_stats))
    stat_index = jnp.arange(row_devices * tok_dev, dtype=jnp.int32)
    starts, offset, doc_rank = doc_tables(doc_lengths, doc_owner)
    owner_index = lax.axis_index("rows")
    every_owner = jnp.arange(row_devices, dtype=jnp.int32)
    tables = jax.vmap(
        lambda owner_value: slot_table(
            owner_value, starts, offset, doc_rank, doc_lengths, doc_owner, CAP
        )
    )(every_owner)
    owner_laid = tuple((jnp.take(values, jnp.take(stat_index, tables[0])) for values in statistics))
    arrived = lax.all_to_all(owner_laid, "rows", split_axis=0, concat_axis=0, tiled=True)
    own_stats = merged_2(fold_sources(arrived), "vocab", combine_stats)
    slot_token, slot_filled, slot_doc = tuple((table[owner_index] for table in tables))
    policy_lp = own_stats[2] - (own_stats[0] + jnp.log(own_stats[1]))
    reference_lp = own_stats[5] - (own_stats[3] + jnp.log(own_stats[4]))
    slot_mask = jnp.take(all_mask, slot_token) * slot_filled
    token_logprob = jnp.where(slot_mask == 1, policy_lp, 0.0)
    reward, counts = document_rewards(
        policy_lp,
        reference_lp,
        slot_mask,
        slot_doc,
        owner_index,
        doc_owner,
        doc_rank,
        doc_score,
        DOC_DEV,
    )
    weighted, token_total = lax.psum((jnp.sum(counts * reward), jnp.sum(counts)), "rows")
    return (token_logprob, reward - weighted / token_total)


def solution(mesh):
    return jax.shard_map(
        per_device,
        mesh=mesh,
        in_specs=(
            P("rows", "vocab"),
            P("rows", "vocab"),
            P(),
            P(),
            P(None, ("rows", "vocab")),
            P(None, ("rows", "vocab")),
            P("rows"),
            P("rows"),
            P(),
            P(),
            P(),
        ),
        out_specs=(P("rows"), P("rows")),
        check_vma=False,
    )
```

profile of v0, /device:TPU:0, one launch (start us, length us, event | category | flops | bytes accessed | tf_op | source)
XLA Modules:
  0.0 248.5 jit_solution(12319093220060869671)
XLA Ops:
  7.3 7.2 %all_gather.64 = bf16[64,1536]{1,0:T(8,128)(2,1)S(1)} all-gather(bf16[64,384]{1,0:T(8,128)(2,1)} %param.18), channel_id=1, replica_groups=mesh['rows'=8,'vocab'=4] {'vocab'}, dimensions={1}, use_global_device_ids=true | all-gather | bytes 245760 | tf_op jit(solution)/shard_map/all_gather | solution.py:127
  16.9 5.8 %all_gather.55 = bf16[64,1536]{1,0:T(8,128)(2,1)S(1)} all-gather(bf16[64,384]{1,0:T(8,128)(2,1)} %param.17), channel_id=1, replica_groups=mesh['rows'=8,'vocab'=4] {'vocab'}, dimensions={1}, use_global_device_ids=true | all-gather | bytes 245760 | tf_op jit(solution)/shard_map/all_gather | solution.py:126
  26.2 6.9 %gather_fusion.1 = s32[1024]{0:T(1024)S(1)} fusion(s32[512]{0:T(512)S(1)} %iota.44, s32[1024]{0:T(1024)S(1)} %bitcast_clamp_fusion.1), kind=kCustom, calls=%fused_computation.clone | custom fusion | bytes 12288 | tf_op jit(solution)/shard_map/jit(_take)/gather | solution.py:157
  33.1 11.8 %all-reduce.2 = (s32[512]{0:T(512)S(1)}, s32[512]{0:T(512)S(1)}) all-reduce(s32[512]{0:T(512)S(1)} %dynamic-update-slice, s32[512]{0:T(512)S(1)} %dynamic-update-slice.1), channel_id=1, replica_groups=mesh['rows'=8,'vocab'=4] {'rows'}, use_global_device_ids=true, to_apply=%add | all-reduce | flops 1024 | bytes 8192
  46.3 15.7 %all-gather.17.cloned.1.call-done = bf16[512,1536]{1,0:T(8,128)(2,1)} async-done(((bf16[64,1536]{1,0:T(8,128)(2,1)}), bf16[512,1536]{1,0:T(8,128)(2,1)}) %all-gather.17.cloned.1.call-update) | async-done | bytes 1572880 | tf_op jit(solution)/shard_map/all_gather | solution.py:142
  64.5 6.9 %gather_fusion.5 = f32[1024]{0:T(1024)S(1)} fusion(f32[512]{0:T(512)S(1)} %get-tuple-element.386, s32[1024]{0:T(1024)S(1)} %bitcast_clamp_fusion), kind=kCustom, calls=%fused_computation.4.clone | custom fusion | bytes 12288 | tf_op jit(solution)/shard_map/jit(_take)/gather | solution.py:157
  71.4 35.4 %all-gather.15.cloned.1.call-done = bf16[512,1536]{1,0:T(8,128)(2,1)} async-done(((bf16[64,1536]{1,0:T(8,128)(2,1)}), bf16[512,1536]{1,0:T(8,128)(2,1)}) %all-gather.15.cloned.1.call-update) | async-done | bytes 1572880 | tf_op jit(solution)/shard_map/all_gather | solution.py:137
  110.7 6.8 %gather_fusion.2 = f32[1024]{0:T(1024)S(1)} fusion(f32[512]{0:T(512)S(1)} %get-tuple-element.388, s32[1024]{0:T(1024)S(1)} %bitcast_clamp_fusion), kind=kCustom, calls=%fused_computation.1.clone | custom fusion | bytes 12288 | tf_op jit(solution)/shard_map/jit(_take)/gather | solution.py:157
  119.3 6.9 %gather_fusion.7 = f32[1024]{0:T(1024)S(1)} fusion(f32[512]{0:T(512)S(1)} %get-tuple-element.323, s32[1024]{0:T(1024)S(1)} %bitcast_clamp_fusion), kind=kCustom, calls=%fused_computation.6.clone | custom fusion | bytes 12288 | tf_op jit(solution)/shard_map/jit(_take)/gather | solution.py:157
  126.7 6.8 %gather_fusion.6 = f32[1024]{0:T(1024)S(1)} fusion(f32[512]{0:T(512)S(1)} %get-tuple-element.324, s32[1024]{0:T(1024)S(1)} %bitcast_clamp_fusion), kind=kCustom, calls=%fused_computation.5.clone | custom fusion | bytes 12288 | tf_op jit(solution)/shard_map/jit(_take)/gather | solution.py:157
  133.6 6.9 %gather_fusion.4 = f32[1024]{0:T(1024)S(1)} fusion(f32[512]{0:T(512)S(1)} %get-tuple-element.331, s32[1024]{0:T(1024)S(1)} %bitcast_clamp_fusion), kind=kCustom, calls=%fused_computation.3.clone | custom fusion | bytes 12288 | tf_op jit(solution)/shard_map/jit(_take)/gather | solution.py:157
  140.5 6.9 %gather_fusion.3 = f32[1024]{0:T(1024)S(1)} fusion(f32[512]{0:T(512)S(1)} %get-tuple-element.330, s32[1024]{0:T(1024)S(1)} %bitcast_clamp_fusion), kind=kCustom, calls=%fused_computation.2.clone | custom fusion | bytes 12288 | tf_op jit(solution)/shard_map/jit(_take)/gather | solution.py:157
  151.4 6.3 %all-to-all-done = f32[8,1,128]{2,1,0:T(1,128)S(1)} async-done(((f32[8,1,128]{2,1,0:T(1,128)}), f32[8,1,128]{2,1,0:T(1,128)S(1)}, u32[]{:S(2)}, u32[]{:S(2)}) %all-to-all-start) | async-done | bytes 4128 | tf_op jit(solution)/shard_map/all_to_all | solution.py:158
  161.0 5.1 %all-gather.6 = f32[4,1,128]{2,1,0:T(1,128)S(1)} all-gather(f32[1,1,128]{2,1,0:T(1,128)S(1)} %bitcast.150), channel_id=2, replica_groups=mesh['rows'=8,'vocab'=4] {'vocab'}, dimensions={0}, use_global_device_ids=true | all-gather | bytes 2560 | tf_op jit(solution)/shard_map/all_gather | solution.py:13
  167.4 4.6 %all-to-all-start.2 = ((f32[8,1,128]{2,1,0:T(1,128)}), f32[8,1,128]{2,1,0:T(1,128)S(1)}, u32[]{:S(2)}, u32[]{:S(2)}) async-start(f32[8,1,128]{2,1,0:T(1,128)} %bitcast.31), calls=%async_computation.2 | async-start | bytes 8192 | tf_op jit(solution)/shard_map/all_to_all | solution.py:158
  172.0 5.1 %all-gather.7 = f32[4,1,128]{2,1,0:T(1,128)S(1)} all-gather(f32[1,1,128]{2,1,0:T(1,128)S(1)} %bitcast.151), channel_id=3, replica_groups=mesh['rows'=8,'vocab'=4] {'vocab'}, dimensions={0}, use_global_device_ids=true | all-gather | bytes 2560 | tf_op jit(solution)/shard_map/all_gather | solution.py:13
  178.5 4.6 %all-to-all-start.3 = ((f32[8,1,128]{2,1,0:T(1,128)}), f32[8,1,128]{2,1,0:T(1,128)S(1)}, u32[]{:S(2)}, u32[]{:S(2)}) async-start(f32[8,1,128]{2,1,0:T(1,128)} %bitcast.37), calls=%async_computation.3 | async-start | bytes 8192 | tf_op jit(solution)/shard_map/all_to_all | solution.py:158
  183.1 5.1 %all-gather.8 = f32[4,1,128]{2,1,0:T(1,128)S(1)} all-gather(f32[1,1,128]{2,1,0:T(1,128)S(1)} %bitcast.154), channel_id=4, replica_groups=mesh['rows'=8,'vocab'=4] {'vocab'}, dimensions={0}, use_global_device_ids=true | all-gather | bytes 2560 | tf_op jit(solution)/shard_map/all_gather | solution.py:13
  189.5 4.6 %all-to-all-start.4 = ((f32[8,1,128]{2,1,0:T(1,128)}), f32[8,1,128]{2,1,0:T(1,128)S(1)}, u32[]{:S(2)}, u32[]{:S(2)}) async-start(f32[8,1,128]{2,1,0:T(1,128)} %bitcast.43), calls=%async_computation.4 | async-start | bytes 8192 | tf_op jit(solution)/shard_map/all_to_all | solution.py:158
  194.2 5.1 %all-gather.9 = f32[4,1,128]{2,1,0:T(1,128)S(1)} all-gather(f32[1,1,128]{2,1,0:T(1,128)S(1)} %bitcast.149), channel_id=5, replica_groups=mesh['rows'=8,'vocab'=4] {'vocab'}, dimensions={0}, use_global_device_ids=true | all-gather | bytes 2560 | tf_op jit(solution)/shard_map/all_gather | solution.py:13
  200.6 4.6 %all-to-all-start.5 = ((f32[8,1,128]{2,1,0:T(1,128)}), f32[8,1,128]{2,1,0:T(1,128)S(1)}, u32[]{:S(2)}, u32[]{:S(2)}) async-start(f32[8,1,128]{2,1,0:T(1,128)} %bitcast.51), calls=%async_computation.5 | async-start | bytes 8192 | tf_op jit(solution)/shard_map/all_to_all | solution.py:158
  205.2 5.1 %all-gather.10 = f32[4,1,128]{2,1,0:T(1,128)S(1)} all-gather(f32[1,1,128]{2,1,0:T(1,128)S(1)} %bitcast.152), channel_id=6, replica_groups=mesh['rows'=8,'vocab'=4] {'vocab'}, dimensions={0}, use_global_device_ids=true | all-gather | bytes 2560 | tf_op jit(solution)/shard_map/all_gather | solution.py:13
  211.7 5.1 %all-gather.11 = f32[4,1,128]{2,1,0:T(1,128)S(1)} all-gather(f32[1,1,128]{2,1,0:T(1,128)S(1)} %bitcast.153), channel_id=7, replica_groups=mesh['rows'=8,'vocab'=4] {'vocab'}, dimensions={0}, use_global_device_ids=true | all-gather | bytes 2560 | tf_op jit(solution)/shard_map/all_gather | solution.py:13
  218.8 21.0 %all-reduce.3 = (f32[]{:T(128)}, f32[]{:T(128)}) all-reduce(f32[]{:T(128)} %get-tuple-element.371, f32[]{:T(128)} %get-tuple-element.332), channel_id=1, replica_groups=mesh['rows'=8,'vocab'=4] {'rows'}, use_global_device_ids=true, to_apply=%region_26.29 | all-reduce | flops 2 | bytes 16 | tf_op jit(solution)/shard_map/psum | solution.py:176
  (87 shorter events, 32.4 us)
Async XLA Ops:
  7.2 54.9 %copy-start = (bf16[1536,512]{1,0:T(8,128)(2,1)S(1)}, bf16[1536,512]{1,0:T(8,128)(2,1)}, u32[]{:S(2)}) copy-start(bf16[1536,512]{1,0:T(8,128)(2,1)} %param.22) | copy-start | bytes 4718596
  7.2 16.8 %copy-start.6 = (u32[32]{0:T(128)S(1)}, u32[32]{0:T(128)}, u32[]{:S(2)}) copy-start(u32[32]{0:T(128)} %constant.141) | copy-start | bytes 388
  7.2 16.5 %copy-start.2 = (s32[16]{0:T(128)S(1)}, s32[16]{0:T(128)}, u32[]{:S(2)}) copy-start(s32[16]{0:T(128)} %param.26) | copy-start | bytes 196
  7.2 16.5 %copy-start.1 = (s32[16]{0:T(128)S(1)}, s32[16]{0:T(128)}, u32[]{:S(2)}) copy-start(s32[16]{0:T(128)} %param.25) | copy-start | bytes 196
  7.2 18.0 %copy-start.4 = (s32[64]{0:T(128)S(1)}, s32[64]{0:T(128)}, u32[]{:S(2)}) copy-start(s32[64]{0:T(128)} %param.24) | copy-start | bytes 772
  7.2 18.2 %copy-start.5 = (s32[64]{0:T(128)S(1)}, s32[64]{0:T(128)}, u32[]{:S(2)}) copy-start(s32[64]{0:T(128)} %param.23) | copy-start | bytes 772
  7.2 54.8 %all-gather.17.cloned.1.call-start = ((), (), s32[]{:S(2)}) async-start(), calls=%async_computation.7 | async-start | bytes 1769472 | tf_op jit(solution)/shard_map/all_gather | solution.py:142
  16.2 90.6 %all-gather.15.cloned.1.call-start = ((), (), s32[]{:S(2)}) async-start(), calls=%async_computation.6 | async-start | bytes 1769472 | tf_op jit(solution)/shard_map/all_gather | solution.py:137
  140.5 10.8 %copy-start.3 = (f32[16]{0:T(128)S(1)}, f32[16]{0:T(128)}, u32[]{:S(2)}) copy-start(f32[16]{0:T(128)} %param.27) | copy-start | bytes 196
  148.0 9.7 %all-to-all-start = ((f32[8,1,128]{2,1,0:T(1,128)}), f32[8,1,128]{2,1,0:T(1,128)S(1)}, u32[]{:S(2)}, u32[]{:S(2)}) async-start(f32[8,1,128]{2,1,0:T(1,128)} %bitcast.17), calls=%async_computation | async-start | bytes 8192 | tf_op jit(solution)/shard_map/all_to_all | solution.py:158
  157.7 9.7 %all-to-all-start.1 = ((f32[8,1,128]{2,1,0:T(1,128)}), f32[8,1,128]{2,1,0:T(1,128)S(1)}, u32[]{:S(2)}, u32[]{:S(2)}) async-start(f32[8,1,128]{2,1,0:T(1,128)} %bitcast.23), calls=%async_computation.1 | async-start | bytes 8192 | tf_op jit(solution)/shard_map/all_to_all | solution.py:158
  167.4 11.1 %all-to-all-start.2 = ((f32[8,1,128]{2,1,0:T(1,128)}), f32[8,1,128]{2,1,0:T(1,128)S(1)}, u32[]{:S(2)}, u32[]{:S(2)}) async-start(f32[8,1,128]{2,1,0:T(1,128)} %bitcast.31), calls=%async_computation.2 | async-start | bytes 8192 | tf_op jit(solution)/shard_map/all_to_all | solution.py:158
  178.5 11.1 %all-to-all-start.3 = ((f32[8,1,128]{2,1,0:T(1,128)}), f32[8,1,128]{2,1,0:T(1,128)S(1)}, u32[]{:S(2)}, u32[]{:S(2)}) async-start(f32[8,1,128]{2,1,0:T(1,128)} %bitcast.37), calls=%async_computation.3 | async-start | bytes 8192 | tf_op jit(solution)/shard_map/all_to_all | solution.py:158
  189.5 11.1 %all-to-all-start.4 = ((f32[8,1,128]{2,1,0:T(1,128)}), f32[8,1,128]{2,1,0:T(1,128)S(1)}, u32[]{:S(2)}, u32[]{:S(2)}) async-start(f32[8,1,128]{2,1,0:T(1,128)} %bitcast.43), calls=%async_computation.4 | async-start | bytes 8192 | tf_op jit(solution)/shard_map/all_to_all | solution.py:158
  200.6 11.1 %all-to-all-start.5 = ((f32[8,1,128]{2,1,0:T(1,128)}), f32[8,1,128]{2,1,0:T(1,128)S(1)}, u32[]{:S(2)}, u32[]{:S(2)}) async-start(f32[8,1,128]{2,1,0:T(1,128)} %bitcast.51), calls=%async_computation.5 | async-start | bytes 8192 | tf_op jit(solution)/shard_map/all_to_all | solution.py:158
Sparse Core Ops, SparseCore 0:
  16.3 45.7 all-gather.16
  64.2 42.5 all-gather.14
where the time goes:
time: 249 us; the launch traced here: 248 us
  blocking collectives  76.2 us (31%)
  waiting for transfers between devices  64.5 us (26%)
  local copies, waits for them, and re-layouts  50.4 us (20%)
  starting transfers between devices  25 us (10%)
  between operations  16.2 us (7%)
  other arithmetic  9.76 us (4%)
  matrix products  6.31 us (3%)
    gather x6, local copies, waits for them, and re-layouts, per_device(): jnp.take(values, jnp.take(stat_index, tables[0]))  41.1 us
    all_gather x1, waiting for transfers between devices, per_device(): lax.all_gather(normed_policy, 'rows', axis=0, tiled=True)  35.4 us
    all_gather x6, blocking collectives, merged_2(): gathered = jax.tree.map(lambda a: lax.all_gather(a, axis), part)  30.3 us
    all_to_all x6, starting transfers between devices, per_device(): lax.all_to_all(owner_laid, 'rows', split_axis=0, concat_axis=0, tiled=True)  24.9 us
    psum x1, blocking collectives, per_device(): lax.psum((jnp.sum(counts * reward), jnp.sum(counts)), 'rows')  21 us
    all_gather x1, waiting for transfers between devices, per_device(): lax.all_gather(normed_reference, 'rows', axis=0, tiled=True)  15.7 us
    all_to_all x6, waiting for transfers between devices, per_device(): lax.all_to_all(owner_laid, 'rows', split_axis=0, concat_axis=0, tiled=True)  13.3 us
    unnamed x1, blocking collectives  11.8 us
  transfers between devices with their start and end apart: 8, of which 8 were waited for; matrix products, arithmetic and copies ran while one was open for 9% of the time, Pallas kernels for 0%

commit v1 on v0

--- a/solution.py
+++ b/solution.py
@@ -134,7 +134,9 @@
     )
     column_base = lax.axis_index(("rows", "vocab")) * head_policy.shape[1]
     piece_stats = column_stats(
-        lax.all_gather(normed_policy, "rows", axis=0, tiled=True),
+        jnp.concatenate(
+            lax.all_to_all(jnp.stack([normed_policy] * lax.axis_size("rows")), "rows", 0, 0), axis=0
+        ),
         head_policy,
         all_targets,
         column_base,

time: 249 us -> 235 us (0.944)
  waiting for transfers between devices: 64.5 us -> 28.7 us
  blocking collectives: 76.2 us -> 93.5 us
  starting transfers between devices: 25 us -> 29.8 us
    all_gather x1 -> x0, waiting for transfers between devices: 35.4 us -> none  [per_device(): lax.all_gather(normed_policy, 'rows', axis=0, tiled=True)]
    unnamed x1, blocking collectives: 11.8 us -> 27.9 us
    all_gather x1, waiting for transfers between devices: 15.7 us -> 8.24 us  [per_device(): lax.all_gather(normed_reference, 'rows', axis=0, tiled=True)]
    all_to_all x6, waiting for transfers between devices: 13.3 us -> 20.5 us  [per_device(): lax.all_to_all(owner_laid, 'rows', split_axis=0, concat_axis=0, tiled=True)]
    all_to_all x0 -> x1, starting transfers between devices: none -> 6.19 us  [per_device(): lax.all_to_all(jnp.stack([normed_policy] * lax.axis_size('rows')), 'rows'...]
  transfers between devices with their start and end apart: 8 -> 8, of which waited for: 8 -> 5; matrix products, arithmetic and copies ran while one was open for 9% -> 9% of each run, Pallas kernels for 0% -> 0%
where the time goes in v1:
time: 235 us; the launch traced here: 234 us
  blocking collectives  93.5 us (40%)
  local copies, waits for them, and re-layouts  51.7 us (22%)
  starting transfers between devices  29.8 us (13%)
  waiting for transfers between devices  28.7 us (12%)
  between operations  16.3 us (7%)
  other arithmetic  8.37 us (4%)
  matrix products  5.9 us (3%)
    gather x6, local copies, waits for them, and re-layouts, per_device(): jnp.take(values, jnp.take(stat_index, tables[0]))  41.1 us
    all_gather x6, blocking collectives, merged_2(): gathered = jax.tree.map(lambda a: lax.all_gather(a, axis), part)  30.3 us
    unnamed x1, blocking collectives  27.9 us
    all_to_all x6, starting transfers between devices, per_device(): lax.all_to_all(owner_laid, 'rows', split_axis=0, concat_axis=0, tiled=True)  23.6 us
    psum x1, blocking collectives, per_device(): lax.psum((jnp.sum(counts * reward), jnp.sum(counts)), 'rows')  22.5 us
    all_to_all x6, waiting for transfers between devices, per_device(): lax.all_to_all(owner_laid, 'rows', split_axis=0, concat_axis=0, tiled=True)  20.5 us
    all_gather x1, waiting for transfers between devices, per_device(): lax.all_gather(normed_reference, 'rows', axis=0, tiled=True)  8.24 us
    all_gather x1, blocking collectives, per_device(): lax.all_gather(hidden_policy, 'vocab', axis=1, tiled=True)  7.21 us
  transfers between devices with their start and end apart: 8, of which 5 were waited for; matrix products, arithmetic and copies ran while one was open for 9% of the time, Pallas kernels for 0%

profile of v1, /device:TPU:0, one launch (start us, length us, event | category | flops | bytes accessed | tf_op | source)
XLA Modules:
  0.0 234.4 jit_solution(3213447427334316278)
XLA Ops:
  7.2 7.2 %all_gather.52 = bf16[64,1536]{1,0:T(8,128)(2,1)S(1)} all-gather(bf16[64,384]{1,0:T(8,128)(2,1)} %param.17), channel_id=1, replica_groups=mesh['rows'=8,'vocab'=4] {'vocab'}, dimensions={1}, use_global_device_ids=true | all-gather | bytes 245760 | tf_op jit(solution)/shard_map/all_gather | solution.py:126
  16.6 6.2 %all-to-all-start = ((bf16[8,64,1536]{2,1,0:T(8,128)(2,1)}), bf16[8,64,1536]{2,1,0:T(8,128)(2,1)S(1)}, u32[]{:S(2)}, u32[]{:S(2)}) async-start(bf16[8,64,1536]{2,1,0:T(8,128)(2,1)} %stack.2), calls=%async_computation | async-start | bytes 3145728 | tf_op jit(solution)/shard_map/all_to_all | solution.py:138
  22.9 5.6 %all_gather.60 = bf16[64,1536]{1,0:T(8,128)(2,1)S(1)} all-gather(bf16[64,384]{1,0:T(8,128)(2,1)S(1)} %copy-done.2), channel_id=1, replica_groups=mesh['rows'=8,'vocab'=4] {'vocab'}, dimensions={1}, use_global_device_ids=true | all-gather | bytes 245760 | tf_op jit(solution)/shard_map/all_gather | solution.py:127
  30.3 6.9 %gather_fusion.1 = s32[1024]{0:T(1024)S(1)} fusion(s32[512]{0:T(512)S(1)} %iota.44, s32[1024]{0:T(1024)S(1)} %bitcast_clamp_fusion.1), kind=kCustom, calls=%fused_computation.clone | custom fusion | bytes 12288 | tf_op jit(solution)/shard_map/jit(_take)/gather | solution.py:159
  38.9 27.9 %all-reduce.2 = (s32[512]{0:T(512)S(1)}, s32[512]{0:T(512)S(1)}) all-reduce(s32[512]{0:T(512)S(1)} %dynamic-update-slice, s32[512]{0:T(512)S(1)} %dynamic-update-slice.1), channel_id=1, replica_groups=mesh['rows'=8,'vocab'=4] {'rows'}, use_global_device_ids=true, to_apply=%add | all-reduce | flops 1024 | bytes 8192
  70.3 6.8 %gather_fusion.2 = f32[1024]{0:T(1024)S(1)} fusion(f32[512]{0:T(512)S(1)} %get-tuple-element.388, s32[1024]{0:T(1024)S(1)} %bitcast_clamp_fusion), kind=kCustom, calls=%fused_computation.1.clone | custom fusion | bytes 12288 | tf_op jit(solution)/shard_map/jit(_take)/gather | solution.py:159
  77.1 8.2 %all-gather.14.cloned.1.call-done = bf16[512,1536]{1,0:T(8,128)(2,1)} async-done(((bf16[64,1536]{1,0:T(8,128)(2,1)}), bf16[512,1536]{1,0:T(8,128)(2,1)}) %all-gather.14.cloned.1.call-update) | async-done | bytes 1572880 | tf_op jit(solution)/shard_map/all_gather | solution.py:144
  89.3 6.8 %gather_fusion.5 = f32[1024]{0:T(1024)S(1)} fusion(f32[512]{0:T(512)S(1)} %get-tuple-element.386, s32[1024]{0:T(1024)S(1)} %bitcast_clamp_fusion), kind=kCustom, calls=%fused_computation.4.clone | custom fusion | bytes 12288 | tf_op jit(solution)/shard_map/jit(_take)/gather | solution.py:159
  97.8 6.9 %gather_fusion.7 = f32[1024]{0:T(1024)S(1)} fusion(f32[512]{0:T(512)S(1)} %get-tuple-element.323, s32[1024]{0:T(1024)S(1)} %bitcast_clamp_fusion), kind=kCustom, calls=%fused_computation.6.clone | custom fusion | bytes 12288 | tf_op jit(solution)/shard_map/jit(_take)/gather | solution.py:159
  105.3 6.8 %gather_fusion.3 = f32[1024]{0:T(1024)S(1)} fusion(f32[512]{0:T(512)S(1)} %get-tuple-element.330, s32[1024]{0:T(1024)S(1)} %bitcast_clamp_fusion), kind=kCustom, calls=%fused_computation.2.clone | custom fusion | bytes 12288 | tf_op jit(solution)/shard_map/jit(_take)/gather | solution.py:159
  112.2 6.9 %gather_fusion.4 = f32[1024]{0:T(1024)S(1)} fusion(f32[512]{0:T(512)S(1)} %get-tuple-element.331, s32[1024]{0:T(1024)S(1)} %bitcast_clamp_fusion), kind=kCustom, calls=%fused_computation.3.clone | custom fusion | bytes 12288 | tf_op jit(solution)/shard_map/jit(_take)/gather | solution.py:159
  119.0 6.9 %gather_fusion.6 = f32[1024]{0:T(1024)S(1)} fusion(f32[512]{0:T(512)S(1)} %get-tuple-element.324, s32[1024]{0:T(1024)S(1)} %bitcast_clamp_fusion), kind=kCustom, calls=%fused_computation.5.clone | custom fusion | bytes 12288 | tf_op jit(solution)/shard_map/jit(_take)/gather | solution.py:159
  129.8 6.4 %all-to-all-done.4 = f32[8,1,128]{2,1,0:T(1,128)S(1)} async-done(((f32[8,1,128]{2,1,0:T(1,128)}), f32[8,1,128]{2,1,0:T(1,128)S(1)}, u32[]{:S(2)}, u32[]{:S(2)}) %all-to-all-start.4) | async-done | bytes 4128 | tf_op jit(solution)/shard_map/all_to_all | solution.py:160
  139.6 6.3 %all-to-all-done.5 = f32[8,1,128]{2,1,0:T(1,128)S(1)} async-done(((f32[8,1,128]{2,1,0:T(1,128)}), f32[8,1,128]{2,1,0:T(1,128)S(1)}, u32[]{:S(2)}, u32[]{:S(2)}) %all-to-all-start.5) | async-done | bytes 4128 | tf_op jit(solution)/shard_map/all_to_all | solution.py:160
  149.2 5.1 %all-gather.10 = f32[4,1,128]{2,1,0:T(1,128)S(1)} all-gather(f32[1,1,128]{2,1,0:T(1,128)S(1)} %bitcast.153), channel_id=6, replica_groups=mesh['rows'=8,'vocab'=4] {'vocab'}, dimensions={0}, use_global_device_ids=true | all-gather | bytes 2560 | tf_op jit(solution)/shard_map/all_gather | solution.py:13
  155.6 4.6 %all-to-all-start.2 = ((f32[8,1,128]{2,1,0:T(1,128)}), f32[8,1,128]{2,1,0:T(1,128)S(1)}, u32[]{:S(2)}, u32[]{:S(2)}) async-start(f32[8,1,128]{2,1,0:T(1,128)} %bitcast.24), calls=%async_computation.2 | async-start | bytes 8192 | tf_op jit(solution)/shard_map/all_to_all | solution.py:160
  160.2 6.5 %all-to-all-done.2 = f32[8,1,128]{2,1,0:T(1,128)S(1)} async-done(((f32[8,1,128]{2,1,0:T(1,128)}), f32[8,1,128]{2,1,0:T(1,128)S(1)}, u32[]{:S(2)}, u32[]{:S(2)}) %all-to-all-start.2) | async-done | bytes 4128 | tf_op jit(solution)/shard_map/all_to_all | solution.py:160
  170.0 5.1 %all-gather.7 = f32[4,1,128]{2,1,0:T(1,128)S(1)} all-gather(f32[1,1,128]{2,1,0:T(1,128)S(1)} %bitcast.154), channel_id=3, replica_groups=mesh['rows'=8,'vocab'=4] {'vocab'}, dimensions={0}, use_global_device_ids=true | all-gather | bytes 2560 | tf_op jit(solution)/shard_map/all_gather | solution.py:13
  175.1 5.0 %all-gather.9 = f32[4,1,128]{2,1,0:T(1,128)S(1)} all-gather(f32[1,1,128]{2,1,0:T(1,128)S(1)} %bitcast.151), channel_id=5, replica_groups=mesh['rows'=8,'vocab'=4] {'vocab'}, dimensions={0}, use_global_device_ids=true | all-gather | bytes 2560 | tf_op jit(solution)/shard_map/all_gather | solution.py:13
  180.2 5.9 %all-to-all-start.6 = ((f32[8,1,128]{2,1,0:T(1,128)}), f32[8,1,128]{2,1,0:T(1,128)S(1)}, u32[]{:S(2)}, u32[]{:S(2)}) async-start(f32[8,1,128]{2,1,0:T(1,128)} %bitcast.52), calls=%async_computation.6 | async-start | bytes 8192 | tf_op jit(solution)/shard_map/all_to_all | solution.py:160
  186.1 5.1 %all-gather.8 = f32[4,1,128]{2,1,0:T(1,128)S(1)} all-gather(f32[1,1,128]{2,1,0:T(1,128)S(1)} %bitcast.156), channel_id=4, replica_groups=mesh['rows'=8,'vocab'=4] {'vocab'}, dimensions={0}, use_global_device_ids=true | all-gather | bytes 2560 | tf_op jit(solution)/shard_map/all_gather | solution.py:13
  191.2 5.0 %all-gather.6 = f32[4,1,128]{2,1,0:T(1,128)S(1)} all-gather(f32[1,1,128]{2,1,0:T(1,128)S(1)} %bitcast.152), channel_id=2, replica_groups=mesh['rows'=8,'vocab'=4] {'vocab'}, dimensions={0}, use_global_device_ids=true | all-gather | bytes 2560 | tf_op jit(solution)/shard_map/all_gather | solution.py:13
  196.2 5.1 %all-gather.11 = f32[4,1,128]{2,1,0:T(1,128)S(1)} all-gather(f32[1,1,128]{2,1,0:T(1,128)S(1)} %bitcast.155), channel_id=7, replica_groups=mesh['rows'=8,'vocab'=4] {'vocab'}, dimensions={0}, use_global_device_ids=true | all-gather | bytes 2560 | tf_op jit(solution)/shard_map/all_gather | solution.py:13
  203.3 22.5 %all-reduce.3 = (f32[]{:T(128)}, f32[]{:T(128)}) all-reduce(f32[]{:T(128)} %get-tuple-element.371, f32[]{:T(128)} %get-tuple-element.332), channel_id=1, replica_groups=mesh['rows'=8,'vocab'=4] {'rows'}, use_global_device_ids=true, to_apply=%region_26.29 | all-reduce | flops 2 | bytes 16 | tf_op jit(solution)/shard_map/psum | solution.py:178
  (93 shorter events, 32.7 us)
Async XLA Ops:
  7.2 61.1 %copy-start = (bf16[1536,512]{1,0:T(8,128)(2,1)S(1)}, bf16[1536,512]{1,0:T(8,128)(2,1)}, u32[]{:S(2)}) copy-start(bf16[1536,512]{1,0:T(8,128)(2,1)} %param.21) | copy-start | bytes 4718596
  16.6 6.2 %copy-start.2 = (bf16[64,384]{1,0:T(8,128)(2,1)S(1)}, bf16[64,384]{1,0:T(8,128)(2,1)}, u32[]{:S(2)}) copy-start(bf16[64,384]{1,0:T(8,128)(2,1)} %param.18) | copy-start | bytes 147460
  16.6 12.0 %copy-start.4 = (bf16[1536]{0:T(1024)(128)(2,1)S(1)}, bf16[1536]{0:T(1024)(128)(2,1)}, u32[]{:S(2)}) copy-start(bf16[1536]{0:T(1024)(128)(2,1)} %param.20) | copy-start | bytes 9220
  16.6 12.8 %copy-start.3 = (s32[16]{0:T(128)S(1)}, s32[16]{0:T(128)}, u32[]{:S(2)}) copy-start(s32[16]{0:T(128)} %param.25) | copy-start | bytes 196
  16.6 13.1 %copy-start.5 = (s32[16]{0:T(128)S(1)}, s32[16]{0:T(128)}, u32[]{:S(2)}) copy-start(s32[16]{0:T(128)} %param.26) | copy-start | bytes 196
  16.6 51.6 %all-to-all-start = ((bf16[8,64,1536]{2,1,0:T(8,128)(2,1)}), bf16[8,64,1536]{2,1,0:T(8,128)(2,1)S(1)}, u32[]{:S(2)}, u32[]{:S(2)}) async-start(bf16[8,64,1536]{2,1,0:T(8,128)(2,1)} %stack.2), calls=%async_computation | async-start | bytes 3145728 | tf_op jit(solution)/shard_map/all_to_all | solution.py:138
  22.8 62.5 %all-gather.14.cloned.1.call-start = ((), (), s32[]{:S(2)}) async-start(), calls=%async_computation.7 | async-start | bytes 1769472 | tf_op jit(solution)/shard_map/all_gather | solution.py:144
  30.3 6.9 %copy-start.9 = (u32[32]{0:T(128)S(1)}, u32[32]{0:T(128)}, u32[]{:S(2)}) copy-start(u32[32]{0:T(128)} %constant.141) | copy-start | bytes 388
  30.3 8.2 %copy-start.7 = (s32[64]{0:T(128)S(1)}, s32[64]{0:T(128)}, u32[]{:S(2)}) copy-start(s32[64]{0:T(128)} %param.24) | copy-start | bytes 772
  30.3 8.4 %copy-start.8 = (s32[64]{0:T(128)S(1)}, s32[64]{0:T(128)}, u32[]{:S(2)}) copy-start(s32[64]{0:T(128)} %param.23) | copy-start | bytes 772
  89.2 6.9 %copy-start.1 = (f32[512,512]{0,1:T(8,128)S(1)}, f32[512,512]{0,1:T(8,128)}, u32[]{:S(2)}) copy-start(f32[512,512]{0,1:T(8,128)} %get-tuple-element.389) | copy-start | bytes 3145732
  119.0 20.5 %copy-start.6 = (f32[16]{0:T(128)S(1)}, f32[16]{0:T(128)}, u32[]{:S(2)}) copy-start(f32[16]{0:T(128)} %param.27) | copy-start | bytes 196
  126.5 9.7 %all-to-all-start.4 = ((f32[8,1,128]{2,1,0:T(1,128)}), f32[8,1,128]{2,1,0:T(1,128)S(1)}, u32[]{:S(2)}, u32[]{:S(2)}) async-start(f32[8,1,128]{2,1,0:T(1,128)} %bitcast.38), calls=%async_computation.4 | async-start | bytes 8192 | tf_op jit(solution)/shard_map/all_to_all | solution.py:160
  136.2 9.7 %all-to-all-start.5 = ((f32[8,1,128]{2,1,0:T(1,128)}), f32[8,1,128]{2,1,0:T(1,128)S(1)}, u32[]{:S(2)}, u32[]{:S(2)}) async-start(f32[8,1,128]{2,1,0:T(1,128)} %bitcast.44), calls=%async_computation.5 | async-start | bytes 8192 | tf_op jit(solution)/shard_map/all_to_all | solution.py:160
  145.9 9.7 %all-to-all-start.1 = ((f32[8,1,128]{2,1,0:T(1,128)}), f32[8,1,128]{2,1,0:T(1,128)S(1)}, u32[]{:S(2)}, u32[]{:S(2)}) async-start(f32[8,1,128]{2,1,0:T(1,128)} %bitcast.18), calls=%async_computation.1 | async-start | bytes 8192 | tf_op jit(solution)/shard_map/all_to_all | solution.py:160
  155.6 11.1 %all-to-all-start.2 = ((f32[8,1,128]{2,1,0:T(1,128)}), f32[8,1,128]{2,1,0:T(1,128)S(1)}, u32[]{:S(2)}, u32[]{:S(2)}) async-start(f32[8,1,128]{2,1,0:T(1,128)} %bitcast.24), calls=%async_computation.2 | async-start | bytes 8192 | tf_op jit(solution)/shard_map/all_to_all | solution.py:160
  166.7 13.5 %all-to-all-start.3 = ((f32[8,1,128]{2,1,0:T(1,128)}), f32[8,1,128]{2,1,0:T(1,128)S(1)}, u32[]{:S(2)}, u32[]{:S(2)}) async-start(f32[8,1,128]{2,1,0:T(1,128)} %bitcast.32), calls=%async_computation.3 | async-start | bytes 8192 | tf_op jit(solution)/shard_map/all_to_all | solution.py:160
  180.2 16.1 %all-to-all-start.6 = ((f32[8,1,128]{2,1,0:T(1,128)}), f32[8,1,128]{2,1,0:T(1,128)S(1)}, u32[]{:S(2)}, u32[]{:S(2)}) async-start(f32[8,1,128]{2,1,0:T(1,128)} %bitcast.52), calls=%async_computation.6 | async-start | bytes 8192 | tf_op jit(solution)/shard_map/all_to_all | solution.py:160
Sparse Core Ops, SparseCore 0:
  29.6 55.7 all-gather.13
